TPU v7x, 32 devices: a whole 2x2x4 slice. The times are simulated.
32 devices in a mesh: obs: 8 (over z, y), rep: 4 (over x, core).
Axes of the slice: x: 2, y: 2, z: 4, core: 2. Of those that a mesh axis runs over, the one named last changes fastest.
Arguments:
- jacobians: float32 [18, 131072], P(None, ('obs', 'rep')), may hold values from -3 to 3
- residuals: float32 [2, 131072], P(None, ('obs', 'rep')), may hold values from -6 to 6
- camera_local: int32 [131072], P(('obs', 'rep')), may hold values from 0 to 1023
- bucket_counts: int32 [32, 8], P(('obs', 'rep')), may hold values from 1 to 512, as said below
- camera_map: int32 [8192], replicated, may hold values from 0 to 8191, each once
Outputs:
- gradient: float32 [9, 8192], replicated
- camera_blocks: float32 [81, 8192], P(None, 'obs')
Inputs may be any that keep to these rules, and one draw needn't show every extreme that they name: bucket_counts[s, d] counts the leading live slots of bucket d of source block s; exactly one destination d has all 512 slots live from every source block, and every other bucket has at most 256 live slots. A slot in bucket d names camera slot d * 1024 + camera_local. `camera_map`: each camera id appears once.
All inputs are finite; a program needn't handle non-finite values.
Results may differ from a plain program's by a relative error of at most 0.0003.
Values sent between devices are 32-bit elements; how exact they have to be, the bound alone decides.
A program may use at most 192 MiB of HBM per device.

v0:
```python
import math

import jax
import jax.numpy as jnp
from jax import lax
from jax.sharding import PartitionSpec as P

CAM_DEV = 1024


def observation_terms(jacobs, resids):
    leading_row = jacobs[0:9]
    trailing_row = jacobs[9:18]
    gradient_terms = leading_row * resids[0:1] + trailing_row * resids[1:2]
    block_terms = (
        leading_row[:, None] * leading_row[None, :] + trailing_row[:, None] * trailing_row[None, :]
    )
    block_terms = block_terms.reshape((81,) + leading_row.shape[1:])
    return jnp.concatenate([gradient_terms, block_terms], axis=0)


def grouped_sums(jac_flat, res_flat, ids_flat, live_flat, width):
    total = jac_flat.shape[1]
    groups = total // width
    camera_rows = lax.broadcasted_iota(jnp.int32, (CAM_DEV, 1), 0)

    def add_group(index, summed):
        start = index * width
        jac_piece = lax.dynamic_slice_in_dim(jac_flat, start, width, 1)
        res_piece = lax.dynamic_slice_in_dim(res_flat, start, width, 1)
        id_piece = lax.dynamic_slice_in_dim(ids_flat, start, width, 0)
        live_piece = lax.dynamic_slice_in_dim(live_flat, start, width, 0)[None, :]
        terms = observation_terms(jac_piece * live_piece, res_piece * live_piece)
        one_hot = (id_piece[None, :] == camera_rows).astype(jnp.float32)
        added = lax.dot_general(
            terms,
            one_hot,
            (((1,), (1,)), ((), ())),
            precision=lax.Precision.HIGHEST,
            preferred_element_type=jnp.float32,
        )
        return summed + added

    return lax.fori_loop(0, groups, add_group, jnp.zeros((90, CAM_DEV), jnp.float32))


def group_width(senders, width):
    return math.gcd(senders, max(1, 2048 // width)) * width


def local(jacobians, residuals, camera_local, bucket_counts, camera_map):
    senders = lax.axis_size("obs")
    capacity = jacobians.shape[1] // senders
    jac_split = jacobians.reshape(18, senders, capacity)
    res_split = residuals.reshape(2, senders, capacity)
    ids_split = camera_local.reshape(1, senders, capacity)
    counts_here = bucket_counts.reshape(1, senders, 1)
    moved_jac, moved_res = (
        lax.all_to_all(jac_split, "obs", split_axis=1, concat_axis=1, tiled=True),
        lax.all_to_all(res_split, "obs", split_axis=1, concat_axis=1, tiled=True),
    )
    moved_ids, moved_counts = (
        lax.all_to_all(ids_split, "obs", split_axis=1, concat_axis=1, tiled=True),
        lax.all_to_all(counts_here, "obs", split_axis=1, concat_axis=1, tiled=True),
    )
    within = lax.broadcasted_iota(jnp.int32, (1, senders, capacity), 2)
    live_mask = (within < moved_counts).astype(jnp.float32)
    summed = grouped_sums(
        moved_jac.reshape(18, senders * capacity),
        moved_res.reshape(2, senders * capacity),
        moved_ids.reshape(senders * capacity),
        live_mask.reshape(senders * capacity),
        group_width(senders, capacity),
    )
    grad_part = summed[:9]
    block_part = summed[9:]
    grad_owned, blocks_out = lax.psum((grad_part, block_part), "rep")
    grad_slots = lax.all_gather(grad_owned, "obs", axis=1, tiled=True)
    gradient = (
        jnp.zeros(grad_slots.shape, jnp.float32)
        .at[:, camera_map]
        .set(grad_slots, unique_indices=True)
    )
    return (gradient, blocks_out)


def solution(mesh):
    in_specs = (
        P(None, ("obs", "rep")),
        P(None, ("obs", "rep")),
        P(("obs", "rep")),
        P(("obs", "rep"), None),
        P(),
    )
    out_specs = (P(), P(None, "obs"))
    return jax.shard_map(local, mesh=mesh, in_specs=in_specs, out_specs=out_specs, check_vma=False)
```

profile of v0, /device:TPU:0, one launch (start us, length us, event | category | flops | bytes accessed | tf_op | source)
XLA Modules:
  0.0 145.9 jit_solution(17524726978750338318)
XLA Ops:
  7.2 0.7 copy.16
  7.9 13.6 %all_to_all.23 = s32[1,8,1]{2,0,1:T(1,128)S(1)} all-to-all(s32[1,8,1]{2,0,1:T(1,128)S(1)} %copy.16), channel_id=1, replica_groups=mesh['obs'=8,'rep'=4] {'obs'}, dimensions={1} | all-to-all | bytes 64 | tf_op jit(solution)/shard_map/all_to_all | solution.py:64
  21.5 3.3 %all-to-all-start.3 = ((s32[1,8,512]{2,0,1:T(1,128)}), s32[1,8,512]{2,0,1:T(1,128)S(1)}, u32[]{:S(2)}, u32[]{:S(2)}) async-start(s32[1,8,512]{2,0,1:T(1,128)} %bitcast.35), calls=%async_computation.3 | async-start | bytes 32768 | tf_op jit(solution)/shard_map/all_to_all | solution.py:63
  24.8 1.2 copy.19
  26.1 0.9 copy.14
  27.0 4.3 %all-to-all-done.3 = s32[1,8,512]{2,0,1:T(1,128)S(1)} async-done(((s32[1,8,512]{2,0,1:T(1,128)}), s32[1,8,512]{2,0,1:T(1,128)S(1)}, u32[]{:S(2)}, u32[]{:S(2)}) %all-to-all-start.3) | async-done | bytes 16416 | tf_op jit(solution)/shard_map/all_to_all | solution.py:63
  31.3 3.5 %all-to-all-start = ((f32[18,8,512]{2,0,1:T(8,128)}), f32[18,8,512]{2,0,1:T(8,128)S(1)}, u32[]{:S(2)}, u32[]{:S(2)}) async-start(f32[18,8,512]{2,0,1:T(8,128)} %copy.14), calls=%async_computation | async-start | bytes 786432 | tf_op jit(solution)/shard_map/all_to_all | solution.py:59
  34.8 0.8 compare_select_fusion
  35.6 0.2 reduce
  35.8 8.3 %all-to-all-done = f32[18,8,512]{2,0,1:T(8,128)S(1)} async-done(((f32[18,8,512]{2,0,1:T(8,128)}), f32[18,8,512]{2,0,1:T(8,128)S(1)}, u32[]{:S(2)}, u32[]{:S(2)}) %all-to-all-start) | async-done | bytes 294944 | tf_op jit(solution)/shard_map/all_to_all | solution.py:59
  44.1 3.7 %all-to-all-start.2 = ((f32[2,8,512]{2,0,1:T(2,128)}), f32[2,8,512]{2,0,1:T(2,128)S(1)}, u32[]{:S(2)}, u32[]{:S(2)}) async-start(f32[2,8,512]{2,0,1:T(2,128)} %bitcast.34), calls=%async_computation.2 | async-start | bytes 65536 | tf_op jit(solution)/shard_map/all_to_all | solution.py:60
  47.9 0.2 copy.15
  48.1 0.2 copy.20
  48.4 6.1 %all-to-all-done.2 = f32[2,8,512]{2,0,1:T(2,128)S(1)} async-done(((f32[2,8,512]{2,0,1:T(2,128)}), f32[2,8,512]{2,0,1:T(2,128)S(1)}, u32[]{:S(2)}, u32[]{:S(2)}) %all-to-all-start.2) | async-done | bytes 32800 | tf_op jit(solution)/shard_map/all_to_all | solution.py:60
  54.4 9.9 %while.14 = (s32[]{:T(128)}, f32[90,1024]{1,0:T(8,128)S(1)}, f32[18,4096]{1,0:T(8,128)S(1)}, f32[4096]{0:T(1024)S(1)}, f32[2,4096]{1,0:T(2,128)S(1)}, /*index=5*...) while((s32[]{:T(128)}, f32[90,1024]{1,0:T(8,128)S(1)}, ...), condition=%wide.region_1.0_spmd.clone, body=%wide.region_0.0_spmd.clone.sunk | while | flops 2267983872 | bytes 4415669 | solution.py:44
  54.8 4.6 %fusion.17 = f32[90,1024]{1,0:T(8,128)S(1)} fusion(s32[2048]{0:T(1024)S(1)} %dynamic_slice.40, f32[81,2048]{1,0:T(8,128)S(1)} %add.86, f32[9,2048]{1,0:T(8,128)S(1)} %get-tuple-element.221, f32[90,1024]{1,0:T(8,128)S(1)} %get-tuple-element.233, pred[]{:T(512)S(6)} %compare.3), kind=kOutput, calls=%fused_computation.5.clone.1 | convolution fusion | flops 2267389952 | bytes 1482753 | tf_op jit(solution)/shard_map/while/body/eval_jaxpr/dot_general | solution.py:35
  59.8 4.6 %fusion.17 = f32[90,1024]{1,0:T(8,128)S(1)} fusion(s32[2048]{0:T(1024)S(1)} %dynamic_slice.40, f32[81,2048]{1,0:T(8,128)S(1)} %add.86, f32[9,2048]{1,0:T(8,128)S(1)} %get-tuple-element.221, f32[90,1024]{1,0:T(8,128)S(1)} %get-tuple-element.233, pred[]{:T(512)S(6)} %compare.3), kind=kOutput, calls=%fused_computation.5.clone.1 | convolution fusion | flops 2267389952 | bytes 1482753 | tf_op jit(solution)/shard_map/while/body/eval_jaxpr/dot_general | solution.py:35
  64.4 0.8 slice.35
  65.2 11.4 %psum.14 = f32[9,1024]{1,0:T(8,128)S(1)} all-reduce(f32[9,1024]{1,0:T(8,128)S(1)} %slice.34), channel_id=1, replica_groups=mesh['obs'=8,'rep'=4] {'rep'}, use_global_device_ids=true, to_apply=%region_2.0 | all-reduce | flops 9216 | bytes 73728 | tf_op jit(solution)/shard_map/psum | solution.py:77
  76.5 31.6 %all_gather.3 = f32[9,8192]{1,0:T(8,128)S(1)} all-gather(f32[9,1024]{1,0:T(8,128)S(1)} %psum.14), channel_id=1, replica_groups=mesh['obs'=8,'rep'=4] {'obs'}, dimensions={1}, use_global_device_ids=true | all-gather | bytes 331776 | tf_op jit(solution)/shard_map/all_gather | solution.py:78
  108.2 2.6 %copy.17 = f32[8192,9]{1,0:T(8,128)} copy(f32[8192,9]{0,1:T(8,128)S(1)} %bitcast.24) | data formatting | bytes 589824 | tf_op jit(solution)/shard_map/all_gather | solution.py:78
  110.8 23.0 %scatter_custom_fusion = f32[9,8192]{0,1:T(8,128)} fusion(s32[8192]{0:T(1024)S(1)} %compare_select_fusion, f32[8192,9]{1,0:T(8,128)} %copy.17, f32[]{:T(128)} %constant.33.clone.1), kind=kCustom, calls=%fused_computation.14 | custom fusion | bytes 295424 | tf_op jit(solution)/shard_map/scatter | solution.py:82
  133.8 3.5 %copy.18 = f32[9,8192]{1,0:T(8,128)} copy(f32[9,8192]{0,1:T(8,128)} %scatter_custom_fusion) | data formatting | bytes 589824
  137.3 1.7 %copy.29 = f32[81,1024]{1,0:T(8,128)} copy(f32[81,1024]{1,0:T(8,128)} %all-reduce.2.cloned.1.call-done) | data formatting | bytes 663552
  (27 shorter events, 0.9 us)
Async XLA Ops:
  21.5 9.9 %all-to-all-start.3 = ((s32[1,8,512]{2,0,1:T(1,128)}), s32[1,8,512]{2,0,1:T(1,128)S(1)}, u32[]{:S(2)}, u32[]{:S(2)}) async-start(s32[1,8,512]{2,0,1:T(1,128)} %bitcast.35), calls=%async_computation.3 | async-start | bytes 32768 | tf_op jit(solution)/shard_map/all_to_all | solution.py:63
  31.3 12.8 %all-to-all-start = ((f32[18,8,512]{2,0,1:T(8,128)}), f32[18,8,512]{2,0,1:T(8,128)S(1)}, u32[]{:S(2)}, u32[]{:S(2)}) async-start(f32[18,8,512]{2,0,1:T(8,128)} %copy.14), calls=%async_computation | async-start | bytes 786432 | tf_op jit(solution)/shard_map/all_to_all | solution.py:59
  44.1 10.3 %all-to-all-start.2 = ((f32[2,8,512]{2,0,1:T(2,128)}), f32[2,8,512]{2,0,1:T(2,128)S(1)}, u32[]{:S(2)}, u32[]{:S(2)}) async-start(f32[2,8,512]{2,0,1:T(2,128)} %bitcast.34), calls=%async_computation.2 | async-start | bytes 65536 | tf_op jit(solution)/shard_map/all_to_all | solution.py:60
  47.8 89.6 %all-reduce.2.cloned.1.call-start = ((), (), s32[]{:S(2)}) async-start(), calls=%async_computation.4 | async-start | bytes 720896 | tf_op jit(solution)/shard_map/psum | solution.py:77
Sparse Core Ops, SparseCore 0:
  65.3 30.0 all-reduce.1
where the time goes:
time: 146 us
  blocking collectives  56.6 us (39%)
  local copies, waits for them, and re-layouts  35.3 us (24%)
  waiting for transfers between devices  18.7 us (13%)
  between operations  14.1 us (10%)
  starting transfers between devices  10.5 us (7%)
  matrix products  9.11 us (6%)
  other arithmetic  1.46 us (1%)
    all_gather x1, blocking collectives, local(): grad_slots = lax.all_gather(grad_owned, 'obs', axis=1, tiled=True)  31.6 us
    scatter x1, local copies, waits for them, and re-layouts, local(): gradient = jnp.zeros(grad_slots.shape, jnp.float32).at[:, camera_map].set...  23 us
    all_to_all x1, blocking collectives, local(): lax.all_to_all(counts_here, 'obs', split_axis=1, concat_axis=1, tiled=True)  13.6 us
    psum x1, blocking collectives, local(): grad_owned, blocks_out = lax.psum((grad_part, block_part), 'rep')  11.4 us
    dot_general x2, matrix products, add_group(): lax.dot_general(terms, one_hot, (((1,), (1,)), ((), ())), precision=lax.P...  9.11 us
    all_to_all x1, waiting for transfers between devices, local(): lax.all_to_all(jac_split, 'obs', split_axis=1, concat_axis=1, tiled=True)  8.26 us
    unnamed x7, local copies, waits for them, and re-layouts  6.79 us
    all_to_all x1, waiting for transfers between devices, local(): lax.all_to_all(res_split, 'obs', split_axis=1, concat_axis=1, tiled=True)  6.1 us
  transfers between devices with their start and end apart: 4, of which 3 were waited for; matrix products, arithmetic and copies ran while one was open for 23% of the time, Pallas kernels for 0%

commit v1 on v0

v1 whole, which is shorter than its diff:
```python
import functools

import jax
import jax.numpy as jnp
from jax import lax
from jax.experimental import pallas as pl
from jax.experimental.pallas import tpu as pltpu
from jax.sharding import PartitionSpec as P

CAM_DEV = 1024
MESH = pl.DeviceIdType.MESH
F32 = jnp.float32
BF16 = jnp.bfloat16
VMEM = pltpu.VMEM
ROWS = 64
GRAD = 48
LOW = 256


def vspec():
    return pl.BlockSpec(memory_space=VMEM)


def split(value):
    high = value.astype(BF16).astype(F32)
    return high, value - high


def pack_kernel(counts, jac, res, ids, out):
    buckets = counts.shape[1]
    cap = jac.shape[1] // buckets
    out[0:18, :] = jac[...]
    out[18:20, :] = res[...]
    place = lax.broadcasted_iota(jnp.int32, (1, cap), 1)
    for d in range(buckets):
        lanes = slice(d * cap, (d + 1) * cap)
        out[20:21, lanes] = jnp.where(place < counts[0, d], ids[:, lanes], -1).astype(F32)
    out[21:24, :] = jnp.zeros((3, jac.shape[1]), F32)


def exchange_kernel(n, packed, moved, own_sem, send_sem, recv_sem):
    me = lax.axis_index("obs")
    cap = moved.shape[2]
    barrier = pltpu.get_barrier_semaphore()
    for i in range(1, n):
        pl.semaphore_signal(barrier, inc=1, device_id={"obs": lax.rem(me + i, n)}, device_id_type=MESH)
    own = pltpu.make_async_copy(
        packed.at[:, pl.ds(pl.multiple_of(me * cap, cap), cap)], moved.at[me], own_sem
    )
    own.start()
    pl.semaphore_wait(barrier, n - 1)
    copies = []
    for i in range(1, n):
        peer = lax.rem(me + i, n)
        copy = pltpu.make_async_remote_copy(
            src_ref=packed.at[:, pl.ds(pl.multiple_of(peer * cap, cap), cap)],
            dst_ref=moved.at[me],
            send_sem=send_sem.at[i],
            recv_sem=recv_sem.at[i],
            device_id={"obs": peer},
            device_id_type=MESH,
        )
        copy.start()
        copies.append(copy)
    own.wait()
    for copy in copies:
        copy.wait()


def add_block(block, terms, acc):
    cap = block.shape[1]
    lead, trail, res = block[0:9], block[9:18], block[18:20]
    ids = block[20:21].astype(jnp.int32)
    at = 0
    for k in range(9):
        terms[at : at + 9 - k, :] = lead[k : k + 1] * lead[k:9] + trail[k : k + 1] * trail[k:9]
        at += 9 - k
    terms[GRAD : GRAD + 9, :] = lead * res[0:1] + trail * res[1:2]
    high, low = split(terms[...])
    both = jnp.concatenate([high, low], axis=0).astype(BF16)
    rows = lax.broadcasted_iota(jnp.int32, (CAM_DEV, cap), 0)
    one_hot = jnp.where(ids == rows, 1.0, 0.0).astype(BF16)
    added = lax.dot_general(both, one_hot, (((1,), (1,)), ((), ())), preferred_element_type=F32)
    acc[...] += added[:ROWS] + added[ROWS:]


def sums_kernel(moved, acc, terms):
    acc[...] = jnp.zeros_like(acc)
    terms[...] = jnp.zeros_like(terms)

    def body(s, carry):
        add_block(moved[s], terms, acc)
        return carry

    lax.fori_loop(0, moved.shape[0], body, 0)


def reduce_kernel(n, m, part, blocks, grads, landed, total, mine, a_send, a_recv, b_send, b_recv, g_send, g_recv, c_send, c_recv):
    me, rep = lax.axis_index("obs"), lax.axis_index("rep")
    width = total.shape[1]
    barrier = pltpu.get_barrier_semaphore()
    for i in range(1, m):
        pl.semaphore_signal(barrier, inc=1, device_id={"rep": lax.rem(rep + i, m)}, device_id_type=MESH)
    for i in range(1, n):
        pl.semaphore_signal(barrier, inc=1, device_id={"obs": lax.rem(me + i, n)}, device_id_type=MESH)
    pl.semaphore_wait(barrier, n + m - 2)

    def send(src, dst, s, r, axis, peer):
        copy = pltpu.make_async_remote_copy(
            src_ref=src, dst_ref=dst, send_sem=s, recv_sem=r, device_id={axis: peer}, device_id_type=MESH
        )
        copy.start()
        return copy

    first = []
    for i in range(1, m):
        peer = lax.rem(rep + i, m)
        lanes = pl.ds(pl.multiple_of(peer * width, width), width)
        first.append(send(part.at[:, lanes], landed.at[i], a_send.at[i], a_recv.at[i], "rep", peer))
    own = part[:, pl.ds(pl.multiple_of(rep * width, width), width)]
    for copy in first:
        copy.wait()
    for i in range(1, m):
        own = own + landed[i]
    total[...] = own[:GRAD]
    mine[...] = own[GRAD : GRAD + 9]
    grads[rep, me] = own[GRAD : GRAD + 9]
    blocks[rep] = own[:GRAD]
    around, sent = [], []
    for i in range(1, n):
        peer = lax.rem(me + i, n)
        around.append(
            send(mine, grads.at[rep, me], g_send.at[i], g_recv.at[i], "obs", peer)
        )
    for j in range(1, m):
        peer = lax.rem(rep + j, m)
        sent.append(
            send(mine, grads.at[rep, me], c_send.at[j, 0], c_recv.at[j, 0], "rep", peer)
        )
        sent.append(send(total, blocks.at[rep], b_send.at[j], b_recv.at[j], "rep", peer))
    for i in range(1, n):
        around[i - 1].wait_recv()
        source = lax.rem(me - i + n, n)
        for j in range(1, m):
            peer = lax.rem(rep + j, m)
            sent.append(
                send(grads.at[rep, source], grads.at[rep, source], c_send.at[j, i], c_recv.at[j, i], "rep", peer)
            )
    for copy in around:
        copy.wait_send()
    for copy in sent:
        copy.wait()


def finish_kernel(blocks, grads, cmap, gradient, out, acc):
    m, n, _, width = grads.shape
    span = m * width
    cams = n * span
    highs = cams // LOW
    at = 0
    for k in range(9):
        for l in range(k, 9):
            for r in range(m):
                row = blocks[r, at : at + 1, :]
                lanes = slice(r * width, (r + 1) * width)
                out[k * 9 + l : k * 9 + l + 1, lanes] = row
                if l != k:
                    out[l * 9 + k : l * 9 + k + 1, lanes] = row
            at += 1
    acc[...] = jnp.zeros_like(acc)

    def body(o, carry):
        slots = jnp.concatenate([grads[r, o] for r in range(m)], axis=1)
        ids = cmap[:, pl.ds(pl.multiple_of(o * span, span), span)]
        up, down = ids // LOW, lax.rem(ids, LOW)
        one_hot = jnp.where(down == lax.broadcasted_iota(jnp.int32, (LOW, span), 0), 1.0, 0.0).astype(BF16)
        high, low = split(slots)
        top = jnp.concatenate([high[0:8], low[0:8]], axis=0)
        up16 = jnp.broadcast_to(up, (16, span))
        dims = (((1,), (1,)), ((), ()))
        group = 16

        def tiles(g, carry):
            lhs = jnp.concatenate(
                [jnp.where(up16 == g * group + h, top, 0.0).astype(BF16) for h in range(group)], axis=0
            )
            where = pl.ds(pl.multiple_of(g * group * 16, group * 16), group * 16)
            acc[where, :] += lax.dot_general(lhs, one_hot, dims, preferred_element_type=F32)
            return carry

        lax.fori_loop(0, highs // group, tiles, 0)
        mask = up == lax.broadcasted_iota(jnp.int32, (highs, span), 0)
        last = jnp.concatenate([jnp.where(mask, high[8:9], 0.0), jnp.where(mask, low[8:9], 0.0)], axis=0).astype(BF16)
        acc[highs * 16 :, :] += lax.dot_general(last, one_hot, dims, preferred_element_type=F32)
        return carry

    lax.fori_loop(0, n, body, 0)
    for h in range(highs):
        lanes = slice(h * LOW, (h + 1) * LOW)
        gradient[0:8, lanes] = acc[h * 16 : h * 16 + 8, :] + acc[h * 16 + 8 : h * 16 + 16, :]
        ninth = highs * 16 + h
        gradient[8:9, lanes] = acc[ninth : ninth + 1, :] + acc[ninth + highs : ninth + highs + 1, :]


def local(jacobians, residuals, camera_local, bucket_counts, camera_map):
    n, m = lax.axis_size("obs"), lax.axis_size("rep")
    slots = jacobians.shape[1]
    cap = slots // n
    cams = camera_map.shape[0]
    width = CAM_DEV // m
    highs = cams // LOW
    limit = 60 * 1024 * 1024
    params = pltpu.CompilerParams(vmem_limit_bytes=limit)
    packed = pl.pallas_call(
        pack_kernel,
        out_shape=jax.ShapeDtypeStruct((24, slots), F32),
        in_specs=[pl.BlockSpec(memory_space=pltpu.SMEM)] + [vspec()] * 3,
        out_specs=vspec(),
        compiler_params=params,
    )(bucket_counts, jacobians, residuals, camera_local.reshape(1, slots))
    moved = pl.pallas_call(
        functools.partial(exchange_kernel, n),
        out_shape=jax.ShapeDtypeStruct((n, 24, cap), F32),
        in_specs=[vspec()],
        out_specs=vspec(),
        scratch_shapes=[
            pltpu.SemaphoreType.DMA,
            pltpu.SemaphoreType.DMA((n,)),
            pltpu.SemaphoreType.DMA((n,)),
        ],
        compiler_params=pltpu.CompilerParams(collective_id=0, has_side_effects=True, vmem_limit_bytes=limit),
    )(packed)
    part = pl.pallas_call(
        sums_kernel,
        out_shape=jax.ShapeDtypeStruct((ROWS, CAM_DEV), F32),
        in_specs=[vspec()],
        out_specs=vspec(),
        scratch_shapes=[VMEM((ROWS, cap), F32)],
        compiler_params=params,
    )(moved)
    dma = pltpu.SemaphoreType.DMA
    blocks, grads = pl.pallas_call(
        functools.partial(reduce_kernel, n, m),
        out_shape=(jax.ShapeDtypeStruct((m, GRAD, width), F32), jax.ShapeDtypeStruct((m, n, 9, width), F32)),
        in_specs=[vspec()],
        out_specs=(vspec(), vspec()),
        scratch_shapes=[
            VMEM((m, ROWS, width), F32),
            VMEM((GRAD, width), F32),
            VMEM((9, width), F32),
            dma((m,)),
            dma((m,)),
            dma((m,)),
            dma((m,)),
            dma((n,)),
            dma((n,)),
            dma((m, n)),
            dma((m, n)),
        ],
        compiler_params=pltpu.CompilerParams(collective_id=1, has_side_effects=True, vmem_limit_bytes=limit),
    )(part)
    gradient, out = pl.pallas_call(
        finish_kernel,
        out_shape=(jax.ShapeDtypeStruct((9, cams), F32), jax.ShapeDtypeStruct((81, CAM_DEV), F32)),
        in_specs=[vspec()] * 3,
        out_specs=(vspec(), vspec()),
        scratch_shapes=[VMEM((highs * 18, LOW), F32)],
        compiler_params=params,
    )(blocks, grads, camera_map.reshape(1, cams))
    return (gradient, out)


def solution(mesh):
    in_specs = (
        P(None, ("obs", "rep")),
        P(None, ("obs", "rep")),
        P(("obs", "rep")),
        P(("obs", "rep"), None),
        P(),
    )
    out_specs = (P(), P(None, "obs"))
    return jax.shard_map(local, mesh=mesh, in_specs=in_specs, out_specs=out_specs, check_vma=False)
```

time: 146 us -> 57.2 us (0.39)
  blocking collectives: 56.6 us -> 0 us
  Pallas kernels: 0 us -> 56.2 us
  local copies, waits for them, and re-layouts: 35.3 us -> 0 us
  waiting for transfers between devices: 18.7 us -> 0 us
  between operations: 14.1 us -> 0.65 us
  starting transfers between devices: 10.5 us -> 0 us
  matrix products: 9.11 us -> 0 us
  other arithmetic: 1.46 us -> 0 us
    pallas_call x0 -> x5, Pallas kernels: none -> 56.2 us  [the longest x1 23 us: local(): pl.pallas_call(functools.partial(reduce_kernel, n, m), out_shape=(jax.Sha...]
    all_gather x1 -> x0, blocking collectives: 31.6 us -> none  [local(): grad_slots = lax.all_gather(grad_owned, 'obs', axis=1, tiled=True)]
    scatter x1 -> x0, local copies, waits for them, and re-layouts: 23 us -> none  [local(): gradient = jnp.zeros(grad_slots.shape, jnp.float32).at[:, camera_map].set...]
    all_to_all x3 -> x0, waiting for transfers between devices: 18.7 us -> none  [the longest x1 8.26 us: local(): lax.all_to_all(jac_split, 'obs', split_axis=1, concat_axis=1, tiled=True)]
    all_to_all x1 -> x0, blocking collectives: 13.6 us -> none  [local(): lax.all_to_all(counts_here, 'obs', split_axis=1, concat_axis=1, tiled=True)]
    psum x1 -> x0, blocking collectives: 11.4 us -> none  [local(): grad_owned, blocks_out = lax.psum((grad_part, block_part), 'rep')]
    all_to_all x3 -> x0, starting transfers between devices: 10.5 us -> none  [the longest x1 3.66 us: local(): lax.all_to_all(res_split, 'obs', split_axis=1, concat_axis=1, tiled=True)]
    dot_general x2 -> x0, matrix products: 9.11 us -> none  [add_group(): lax.dot_general(terms, one_hot, (((1,), (1,)), ((), ())), precision=lax.P...]
  transfers between devices with their start and end apart: 4 -> 0, of which waited for: 3 -> 0; matrix products, arithmetic and copies ran while one was open for 23% -> 0% of each run, Pallas kernels for 0% -> 0%
where the time goes in v1:
time: 57.2 us; the launch traced here: 56.9 us
  Pallas kernels  56.2 us (98%)
  between operations  0.65 us (1%)
    pallas_call x1, Pallas kernels, local(): pl.pallas_call(functools.partial(reduce_kernel, n, m), out_shape=(jax.Sha...  23 us
    pallas_call x1, Pallas kernels, local(): pl.pallas_call(functools.partial(exchange_kernel, n), out_shape=jax.Shape...  14.2 us
    pallas_call x1, Pallas kernels, local(): pl.pallas_call(finish_kernel, out_shape=(jax.ShapeDtypeStruct((9, cams),...  11 us
    pallas_call x1, Pallas kernels, local(): pl.pallas_call(sums_kernel, out_shape=jax.ShapeDtypeStruct((ROWS, CAM_DEV...  6.17 us
    pallas_call x1, Pallas kernels, local(): pl.pallas_call(pack_kernel, out_shape=jax.ShapeDtypeStruct((24, slots), F...  1.83 us

profile of v1, /device:TPU:0, one launch (start us, length us, event | category | flops | bytes accessed | tf_op | source)
XLA Modules:
  0.0 56.9 jit_solution(5571836452586933169)
XLA Ops:
  0.6 1.8 %shard_map.68.packed = f32[24,4096]{1,0:T(8,128)} custom-call(s32[1,8]{1,0:T(1,128)} %counts.1, f32[18,4096]{1,0:T(8,128)} %jac.1, f32[2,4096]{1,0:T(2,128)} %res.1, s32[1,4096]{1,0:T(1,128)} %bitcast.3), custom_call_target="tpu_custom_call" | custom-call | tf_op jit(solution)/shard_map/pallas_call | solution.py:214
  2.5 14.2 %shard_map.69.moved = f32[8,24,512]{2,1,0:T(8,128)} custom-call(f32[24,4096]{1,0:T(8,128)} %shard_map.68.packed), custom_call_target="tpu_custom_call" | custom-call | tf_op jit(solution)/shard_map/pallas_call | solution.py:221
  16.7 6.2 %shard_map.70.part = f32[64,1024]{1,0:T(8,128)} custom-call(f32[8,24,512]{2,1,0:T(8,128)} %shard_map.69.moved), custom_call_target="tpu_custom_call" | custom-call | tf_op jit(solution)/shard_map/pallas_call | solution.py:233
  22.9 23.0 %shard_map.71 = (f32[4,48,256]{2,1,0:T(8,128)}, f32[4,8,9,256]{3,2,1,0:T(8,128)}) custom-call(f32[64,1024]{1,0:T(8,128)} %shard_map.70.part), custom_call_target="tpu_custom_call" | custom-call | tf_op jit(solution)/shard_map/pallas_call | solution.py:242
  45.9 11.0 %shard_map.72 = (f32[9,8192]{1,0:T(8,128)}, f32[81,1024]{1,0:T(8,128)}) custom-call(f32[4,48,256]{2,1,0:T(8,128)} %get-tuple-element.4.blocks, f32[4,8,9,256]{3,2,1,0:T(8,128)} %get-tuple-element.5.grads, s32[1,8192]{1,0:T(1,128)} %bitcast.2), custom_call_target="tpu_custom_call" | custom-call | tf_op jit(solution)/shard_map/pallas_call | solution.py:262

commit v2 on v1

--- a/solution.py
+++ b/solution.py
@@ -12,8 +12,9 @@
 F32 = jnp.float32
 BF16 = jnp.bfloat16
 VMEM = pltpu.VMEM
-ROWS = 64
-GRAD = 48
+ROWS = 56
+GRAD = 45
+KEPT = 48
 LOW = 256
 
 
@@ -26,7 +27,7 @@
     return high, value - high
 
 
-def pack_kernel(counts, jac, res, ids, out):
+def pack(counts, jac, res, ids, out):
     buckets = counts.shape[1]
     cap = jac.shape[1] // buckets
     out[0:18, :] = jac[...]
@@ -36,35 +37,6 @@
         lanes = slice(d * cap, (d + 1) * cap)
         out[20:21, lanes] = jnp.where(place < counts[0, d], ids[:, lanes], -1).astype(F32)
     out[21:24, :] = jnp.zeros((3, jac.shape[1]), F32)
-
-
-def exchange_kernel(n, packed, moved, own_sem, send_sem, recv_sem):
-    me = lax.axis_index("obs")
-    cap = moved.shape[2]
-    barrier = pltpu.get_barrier_semaphore()
-    for i in range(1, n):
-        pl.semaphore_signal(barrier, inc=1, device_id={"obs": lax.rem(me + i, n)}, device_id_type=MESH)
-    own = pltpu.make_async_copy(
-        packed.at[:, pl.ds(pl.multiple_of(me * cap, cap), cap)], moved.at[me], own_sem
-    )
-    own.start()
-    pl.semaphore_wait(barrier, n - 1)
-    copies = []
-    for i in range(1, n):
-        peer = lax.rem(me + i, n)
-        copy = pltpu.make_async_remote_copy(
-            src_ref=packed.at[:, pl.ds(pl.multiple_of(peer * cap, cap), cap)],
-            dst_ref=moved.at[me],
-            send_sem=send_sem.at[i],
-            recv_sem=recv_sem.at[i],
-            device_id={"obs": peer},
-            device_id_type=MESH,
-        )
-        copy.start()
-        copies.append(copy)
-    own.wait()
-    for copy in copies:
-        copy.wait()
 
 
 def add_block(block, terms, acc):
@@ -84,26 +56,53 @@
     acc[...] += added[:ROWS] + added[ROWS:]
 
 
-def sums_kernel(moved, acc, terms):
-    acc[...] = jnp.zeros_like(acc)
-    terms[...] = jnp.zeros_like(terms)
-
-    def body(s, carry):
-        add_block(moved[s], terms, acc)
-        return carry
-
-    lax.fori_loop(0, moved.shape[0], body, 0)
-
-
-def reduce_kernel(n, m, part, blocks, grads, landed, total, mine, a_send, a_recv, b_send, b_recv, g_send, g_recv, c_send, c_recv):
+def main_kernel(
+    n, m, counts, jac, res, ids, blocks, grads, packed, moved, terms, part, landed, total, mine,
+    x_send, x_recv, a_send, a_recv, b_send, b_recv, g_send, g_recv, c_send, c_recv,
+):
     me, rep = lax.axis_index("obs"), lax.axis_index("rep")
     width = total.shape[1]
+    cap = moved.shape[2]
     barrier = pltpu.get_barrier_semaphore()
+    for i in range(1, n):
+        pl.semaphore_signal(barrier, inc=1, device_id={"obs": lax.rem(me + i, n)}, device_id_type=MESH)
     for i in range(1, m):
         pl.semaphore_signal(barrier, inc=1, device_id={"rep": lax.rem(rep + i, m)}, device_id_type=MESH)
-    for i in range(1, n):
-        pl.semaphore_signal(barrier, inc=1, device_id={"obs": lax.rem(me + i, n)}, device_id_type=MESH)
+    pack(counts, jac, res, ids, packed)
+    part[...] = jnp.zeros_like(part)
+    terms[...] = jnp.zeros_like(terms)
     pl.semaphore_wait(barrier, n + m - 2)
+
+    def lanes_of(peer):
+        return pl.ds(pl.multiple_of(peer * cap, cap), cap)
+
+    def handing(i):
+        peer = lax.rem(me + i, n)
+        return pltpu.make_async_remote_copy(
+            src_ref=packed.at[:, lanes_of(peer)],
+            dst_ref=moved.at[i],
+            send_sem=x_send.at[i],
+            recv_sem=x_recv.at[i],
+            device_id={"obs": peer},
+            device_id_type=MESH,
+        )
+
+    def start(i, carry):
+        handing(i).start()
+        return carry
+
+    def take(i, carry):
+        handing(i).wait_recv()
+        add_block(moved[i], terms, part)
+        return carry
+
+    def drain(i, carry):
+        handing(i).wait_send()
+        return carry
+
+    lax.fori_loop(1, n, start, 0)
+    add_block(packed[:, lanes_of(me)], terms, part)
+    lax.fori_loop(1, n, take, 0)
 
     def send(src, dst, s, r, axis, peer):
         copy = pltpu.make_async_remote_copy(
@@ -117,15 +116,16 @@
         peer = lax.rem(rep + i, m)
         lanes = pl.ds(pl.multiple_of(peer * width, width), width)
         first.append(send(part.at[:, lanes], landed.at[i], a_send.at[i], a_recv.at[i], "rep", peer))
+    lax.fori_loop(1, n, drain, 0)
     own = part[:, pl.ds(pl.multiple_of(rep * width, width), width)]
     for copy in first:
         copy.wait()
     for i in range(1, m):
         own = own + landed[i]
-    total[...] = own[:GRAD]
+    total[...] = own[:KEPT]
     mine[...] = own[GRAD : GRAD + 9]
     grads[rep, me] = own[GRAD : GRAD + 9]
-    blocks[rep] = own[:GRAD]
+    blocks[rep] = own[:KEPT]
     around, sent = [], []
     for i in range(1, n):
         peer = lax.rem(me + i, n)
@@ -211,43 +211,22 @@
     highs = cams // LOW
     limit = 60 * 1024 * 1024
     params = pltpu.CompilerParams(vmem_limit_bytes=limit)
-    packed = pl.pallas_call(
-        pack_kernel,
-        out_shape=jax.ShapeDtypeStruct((24, slots), F32),
-        in_specs=[pl.BlockSpec(memory_space=pltpu.SMEM)] + [vspec()] * 3,
-        out_specs=vspec(),
-        compiler_params=params,
-    )(bucket_counts, jacobians, residuals, camera_local.reshape(1, slots))
-    moved = pl.pallas_call(
-        functools.partial(exchange_kernel, n),
-        out_shape=jax.ShapeDtypeStruct((n, 24, cap), F32),
-        in_specs=[vspec()],
-        out_specs=vspec(),
-        scratch_shapes=[
-            pltpu.SemaphoreType.DMA,
-            pltpu.SemaphoreType.DMA((n,)),
-            pltpu.SemaphoreType.DMA((n,)),
-        ],
-        compiler_params=pltpu.CompilerParams(collective_id=0, has_side_effects=True, vmem_limit_bytes=limit),
-    )(packed)
-    part = pl.pallas_call(
-        sums_kernel,
-        out_shape=jax.ShapeDtypeStruct((ROWS, CAM_DEV), F32),
-        in_specs=[vspec()],
-        out_specs=vspec(),
-        scratch_shapes=[VMEM((ROWS, cap), F32)],
-        compiler_params=params,
-    )(moved)
     dma = pltpu.SemaphoreType.DMA
     blocks, grads = pl.pallas_call(
-        functools.partial(reduce_kernel, n, m),
-        out_shape=(jax.ShapeDtypeStruct((m, GRAD, width), F32), jax.ShapeDtypeStruct((m, n, 9, width), F32)),
-        in_specs=[vspec()],
+        functools.partial(main_kernel, n, m),
+        out_shape=(jax.ShapeDtypeStruct((m, KEPT, width), F32), jax.ShapeDtypeStruct((m, n, 9, width), F32)),
+        in_specs=[pl.BlockSpec(memory_space=pltpu.SMEM)] + [vspec()] * 3,
         out_specs=(vspec(), vspec()),
         scratch_shapes=[
+            VMEM((24, slots), F32),
+            VMEM((n, 24, cap), F32),
+            VMEM((ROWS, cap), F32),
+            VMEM((ROWS, CAM_DEV), F32),
             VMEM((m, ROWS, width), F32),
-            VMEM((GRAD, width), F32),
+            VMEM((KEPT, width), F32),
             VMEM((9, width), F32),
+            dma((n,)),
+            dma((n,)),
             dma((m,)),
             dma((m,)),
             dma((m,)),
@@ -257,8 +236,8 @@
             dma((m, n)),
             dma((m, n)),
         ],
-        compiler_params=pltpu.CompilerParams(collective_id=1, has_side_effects=True, vmem_limit_bytes=limit),
-    )(part)
+        compiler_params=pltpu.CompilerParams(collective_id=0, has_side_effects=True, vmem_limit_bytes=limit),
+    )(bucket_counts, jacobians, residuals, camera_local.reshape(1, slots))
     gradient, out = pl.pallas_call(
         finish_kernel,
         out_shape=(jax.ShapeDtypeStruct((9, cams), F32), jax.ShapeDtypeStruct((81, CAM_DEV), F32)),

time: 57.2 us -> 46.7 us (0.82)
  Pallas kernels: 56.2 us -> 45.9 us
    pallas_call x4 -> x1, Pallas kernels: 45.2 us -> 34.9 us  [local(): pl.pallas_call(functools.partial(main_kernel, n, m), out_shape=(jax.Shape...]
where the time goes in v2:
time: 46.7 us; the launch traced here: 46.5 us
  Pallas kernels  45.9 us (98%)
  between operations  0.64 us (1%)
    pallas_call x1, Pallas kernels, local(): pl.pallas_call(functools.partial(main_kernel, n, m), out_shape=(jax.Shape...  34.9 us
    pallas_call x1, Pallas kernels, local(): pl.pallas_call(finish_kernel, out_shape=(jax.ShapeDtypeStruct((9, cams),...  11 us

profile of v2, /device:TPU:0, one launch (start us, length us, event | category | flops | bytes accessed | tf_op | source)
XLA Modules:
  0.0 46.5 jit_solution(11687570328209451450)
XLA Ops:
  0.6 34.9 %shard_map.68 = (f32[4,48,256]{2,1,0:T(8,128)}, f32[4,8,9,256]{3,2,1,0:T(8,128)}) custom-call(s32[1,8]{1,0:T(1,128)} %counts.1, f32[18,4096]{1,0:T(8,128)} %jac.1, f32[2,4096]{1,0:T(2,128)} %res.1, s32[1,4096]{1,0:T(1,128)} %bitcast.3), custom_call_target="tpu_custom_call" | custom-call | tf_op jit(solution)/shard_map/pallas_call | solution.py:215
  35.5 11.0 %shard_map.69 = (f32[9,8192]{1,0:T(8,128)}, f32[81,1024]{1,0:T(8,128)}) custom-call(f32[4,48,256]{2,1,0:T(8,128)} %get-tuple-element.4.blocks, f32[4,8,9,256]{3,2,1,0:T(8,128)} %get-tuple-element.5.grads, s32[1,8192]{1,0:T(1,128)} %bitcast.2), custom_call_target="tpu_custom_call" | custom-call | tf_op jit(solution)/shard_map/pallas_call | solution.py:241

commit v3 on v2

--- a/solution.py
+++ b/solution.py
@@ -37,6 +37,13 @@
         lanes = slice(d * cap, (d + 1) * cap)
         out[20:21, lanes] = jnp.where(place < counts[0, d], ids[:, lanes], -1).astype(F32)
     out[21:24, :] = jnp.zeros((3, jac.shape[1]), F32)
+
+
+def one_hot_of(low, wide):
+    shape = (wide, low.shape[1])
+    rows = lax.broadcasted_iota(jnp.int32, shape, 0).astype(F32).astype(BF16)
+    there = jnp.broadcast_to(low.astype(F32), shape).astype(BF16)
+    return jnp.where(there == rows, jnp.ones(shape, BF16), jnp.zeros(shape, BF16))
 
 
 def add_block(block, terms, acc):
@@ -50,10 +57,17 @@
     terms[GRAD : GRAD + 9, :] = lead * res[0:1] + trail * res[1:2]
     high, low = split(terms[...])
     both = jnp.concatenate([high, low], axis=0).astype(BF16)
-    rows = lax.broadcasted_iota(jnp.int32, (CAM_DEV, cap), 0)
-    one_hot = jnp.where(ids == rows, 1.0, 0.0).astype(BF16)
-    added = lax.dot_general(both, one_hot, (((1,), (1,)), ((), ())), preferred_element_type=F32)
-    acc[...] += added[:ROWS] + added[ROWS:]
+    pieces, _, width = acc.shape
+    up = jnp.where(ids < 0, -1, ids // width)
+    down = ids - up * width
+    one_hot = one_hot_of(down, width)
+    up = jnp.broadcast_to(up.astype(F32), both.shape).astype(BF16)
+    zero = jnp.zeros_like(both)
+    lhs = jnp.concatenate([jnp.where(up == jnp.asarray(h, BF16), both, zero) for h in range(pieces)], axis=0)
+    added = lax.dot_general(lhs, one_hot, (((1,), (1,)), ((), ())), preferred_element_type=F32)
+    for h in range(pieces):
+        at = h * 2 * ROWS
+        acc[h] += added[at : at + ROWS] + added[at + ROWS : at + 2 * ROWS]
 
 
 def main_kernel(
@@ -114,10 +128,9 @@
     first = []
     for i in range(1, m):
         peer = lax.rem(rep + i, m)
-        lanes = pl.ds(pl.multiple_of(peer * width, width), width)
-        first.append(send(part.at[:, lanes], landed.at[i], a_send.at[i], a_recv.at[i], "rep", peer))
+        first.append(send(part.at[peer], landed.at[i], a_send.at[i], a_recv.at[i], "rep", peer))
     lax.fori_loop(1, n, drain, 0)
-    own = part[:, pl.ds(pl.multiple_of(rep * width, width), width)]
+    own = part[rep]
     for copy in first:
         copy.wait()
     for i in range(1, m):
@@ -173,24 +186,33 @@
         slots = jnp.concatenate([grads[r, o] for r in range(m)], axis=1)
         ids = cmap[:, pl.ds(pl.multiple_of(o * span, span), span)]
         up, down = ids // LOW, lax.rem(ids, LOW)
-        one_hot = jnp.where(down == lax.broadcasted_iota(jnp.int32, (LOW, span), 0), 1.0, 0.0).astype(BF16)
+        one_hot = one_hot_of(down, LOW)
         high, low = split(slots)
-        top = jnp.concatenate([high[0:8], low[0:8]], axis=0)
-        up16 = jnp.broadcast_to(up, (16, span))
+        top = jnp.concatenate([high[0:8], low[0:8]], axis=0).astype(BF16)
+        up16 = jnp.broadcast_to(up.astype(F32), (16, span)).astype(BF16)
+        none = jnp.zeros_like(top)
+        mask = up == lax.broadcasted_iota(jnp.int32, (highs, span), 0)
+        last = jnp.concatenate([jnp.where(mask, high[8:9], 0.0), jnp.where(mask, low[8:9], 0.0)], axis=0).astype(BF16)
         dims = (((1,), (1,)), ((), ()))
-        group = 16
-
-        def tiles(g, carry):
-            lhs = jnp.concatenate(
-                [jnp.where(up16 == g * group + h, top, 0.0).astype(BF16) for h in range(group)], axis=0
-            )
+        group = min(highs, 32)
+
+        def tiles(start):
+            return [
+                jnp.where(up16 == jnp.asarray(start + h, F32).astype(BF16), top, none) for h in range(group)
+            ]
+
+        if group == highs:
+            lhs = jnp.concatenate(tiles(0) + [last], axis=0)
+            acc[...] += lax.dot_general(lhs, one_hot, dims, preferred_element_type=F32)
+            return carry
+
+        def some(g, carry):
+            lhs = jnp.concatenate(tiles(g * group), axis=0)
             where = pl.ds(pl.multiple_of(g * group * 16, group * 16), group * 16)
             acc[where, :] += lax.dot_general(lhs, one_hot, dims, preferred_element_type=F32)
             return carry
 
-        lax.fori_loop(0, highs // group, tiles, 0)
-        mask = up == lax.broadcasted_iota(jnp.int32, (highs, span), 0)
-        last = jnp.concatenate([jnp.where(mask, high[8:9], 0.0), jnp.where(mask, low[8:9], 0.0)], axis=0).astype(BF16)
+        lax.fori_loop(0, highs // group, some, 0)
         acc[highs * 16 :, :] += lax.dot_general(last, one_hot, dims, preferred_element_type=F32)
         return carry
 
@@ -221,7 +243,7 @@
             VMEM((24, slots), F32),
             VMEM((n, 24, cap), F32),
             VMEM((ROWS, cap), F32),
-            VMEM((ROWS, CAM_DEV), F32),
+            VMEM((m, ROWS, width), F32),
             VMEM((m, ROWS, width), F32),
             VMEM((KEPT, width), F32),
             VMEM((9, width), F32),

time: 46.7 us -> 41.4 us (0.89)
  Pallas kernels: 45.9 us -> 40.6 us
    pallas_call x1, Pallas kernels: 11 us -> 6.26 us  [local(): pl.pallas_call(finish_kernel, out_shape=(jax.ShapeDtypeStruct((9, cams),...]
    pallas_call x1, Pallas kernels: 34.9 us -> 34.4 us  [local(): pl.pallas_call(functools.partial(main_kernel, n, m), out_shape=(jax.Shape...]
where the time goes in v3:
time: 41.4 us; the launch traced here: 41.3 us
  Pallas kernels  40.6 us (98%)
  between operations  0.64 us (2%)
    pallas_call x1, Pallas kernels, local(): pl.pallas_call(functools.partial(main_kernel, n, m), out_shape=(jax.Shape...  34.4 us
    pallas_call x1, Pallas kernels, local(): pl.pallas_call(finish_kernel, out_shape=(jax.ShapeDtypeStruct((9, cams),...  6.26 us

profile of v3, /device:TPU:0, one launch (start us, length us, event | category | flops | bytes accessed | tf_op | source)
XLA Modules:
  0.0 41.3 jit_solution(3997405379544925102)
XLA Ops:
  0.6 34.4 %shard_map.68 = (f32[4,48,256]{2,1,0:T(8,128)}, f32[4,8,9,256]{3,2,1,0:T(8,128)}) custom-call(s32[1,8]{1,0:T(1,128)} %counts.1, f32[18,4096]{1,0:T(8,128)} %jac.1, f32[2,4096]{1,0:T(2,128)} %res.1, s32[1,4096]{1,0:T(1,128)} %bitcast.3), custom_call_target="tpu_custom_call" | custom-call | tf_op jit(solution)/shard_map/pallas_call | solution.py:237
  35.0 6.3 %shard_map.69 = (f32[9,8192]{1,0:T(8,128)}, f32[81,1024]{1,0:T(8,128)}) custom-call(f32[4,48,256]{2,1,0:T(8,128)} %get-tuple-element.4.blocks, f32[4,8,9,256]{3,2,1,0:T(8,128)} %get-tuple-element.5.grads, s32[1,8192]{1,0:T(1,128)} %bitcast.2), custom_call_target="tpu_custom_call" | custom-call | tf_op jit(solution)/shard_map/pallas_call | solution.py:263

commit v4 on v3

--- a/solution.py
+++ b/solution.py
@@ -36,7 +36,6 @@
     for d in range(buckets):
         lanes = slice(d * cap, (d + 1) * cap)
         out[20:21, lanes] = jnp.where(place < counts[0, d], ids[:, lanes], -1).astype(F32)
-    out[21:24, :] = jnp.zeros((3, jac.shape[1]), F32)
 
 
 def one_hot_of(low, wide):
@@ -70,8 +69,66 @@
         acc[h] += added[at : at + ROWS] + added[at + ROWS : at + 2 * ROWS]
 
 
+def expand(blocks, out):
+    m, _, width = blocks.shape
+    at = 0
+    for k in range(9):
+        for l in range(k, 9):
+            for r in range(m):
+                row = blocks[r, at : at + 1, :]
+                lanes = slice(r * width, (r + 1) * width)
+                out[k * 9 + l : k * 9 + l + 1, lanes] = row
+                if l != k:
+                    out[l * 9 + k : l * 9 + k + 1, lanes] = row
+            at += 1
+
+
+def place_chunk(o, grads, cmap, ready, acc):
+    m, n, _, width = grads.shape
+    span = m * width
+    highs = n * span // LOW
+    slots = jnp.concatenate([grads[r, o] for r in range(m)], axis=1)
+    ids = cmap[:, pl.ds(pl.multiple_of(o * span, span), span)]
+    up = ids // LOW
+    one_hot = one_hot_of(lax.rem(ids, LOW), LOW) if ready is None else ready[o]
+    high, low = split(slots)
+    top = jnp.concatenate([high[0:8], low[0:8]], axis=0).astype(BF16)
+    up16 = jnp.broadcast_to(up.astype(F32), (16, span)).astype(BF16)
+    none = jnp.zeros_like(top)
+    mask = up == lax.broadcasted_iota(jnp.int32, (highs, span), 0)
+    last = jnp.concatenate([jnp.where(mask, high[8:9], 0.0), jnp.where(mask, low[8:9], 0.0)], axis=0).astype(BF16)
+    dims = (((1,), (1,)), ((), ()))
+    group = min(highs, 32)
+
+    def tiles(start):
+        return [jnp.where(up16 == jnp.asarray(start + h, F32).astype(BF16), top, none) for h in range(group)]
+
+    if group == highs:
+        lhs = jnp.concatenate(tiles(0) + [last], axis=0)
+        acc[...] += lax.dot_general(lhs, one_hot, dims, preferred_element_type=F32)
+        return
+
+    def some(g, carry):
+        lhs = jnp.concatenate(tiles(g * group), axis=0)
+        where = pl.ds(pl.multiple_of(g * group * 16, group * 16), group * 16)
+        acc[where, :] += lax.dot_general(lhs, one_hot, dims, preferred_element_type=F32)
+        return carry
+
+    lax.fori_loop(0, highs // group, some, 0)
+    acc[highs * 16 :, :] += lax.dot_general(last, one_hot, dims, preferred_element_type=F32)
+
+
+def lay_out(acc, gradient):
+    highs = gradient.shape[1] // LOW
+    for h in range(highs):
+        lanes = slice(h * LOW, (h + 1) * LOW)
+        gradient[0:8, lanes] = acc[h * 16 : h * 16 + 8, :] + acc[h * 16 + 8 : h * 16 + 16, :]
+        ninth = highs * 16 + h
+        gradient[8:9, lanes] = acc[ninth : ninth + 1, :] + acc[ninth + highs : ninth + highs + 1, :]
+
+
 def main_kernel(
-    n, m, counts, jac, res, ids, blocks, grads, packed, moved, terms, part, landed, total, mine,
+    n, m, counts, jac, res, ids, cmap, gradient, out, blocks, grads, ready, spread, packed, moved, terms, part, landed, total, mine,
     x_send, x_recv, a_send, a_recv, b_send, b_recv, g_send, g_recv, c_send, c_recv,
 ):
     me, rep = lax.axis_index("obs"), lax.axis_index("rep")
@@ -116,6 +173,17 @@
 
     lax.fori_loop(1, n, start, 0)
     add_block(packed[:, lanes_of(me)], terms, part)
+    early = ready.shape[0] == n
+    span = m * width
+
+    def prepare(o, carry):
+        ids_here = cmap[:, pl.ds(pl.multiple_of(o * span, span), span)]
+        ready[o] = one_hot_of(lax.rem(ids_here, LOW), LOW)
+        return carry
+
+    if early:
+        lax.fori_loop(0, n, prepare, 0)
+    spread[...] = jnp.zeros_like(spread)
     lax.fori_loop(1, n, take, 0)
 
     def send(src, dst, s, r, axis, peer):
@@ -139,89 +207,42 @@
     mine[...] = own[GRAD : GRAD + 9]
     grads[rep, me] = own[GRAD : GRAD + 9]
     blocks[rep] = own[:KEPT]
-    around, sent = [], []
+    around, wide, across = [], [], {}
     for i in range(1, n):
         peer = lax.rem(me + i, n)
-        around.append(
-            send(mine, grads.at[rep, me], g_send.at[i], g_recv.at[i], "obs", peer)
-        )
+        around.append(send(mine, grads.at[rep, me], g_send.at[i], g_recv.at[i], "obs", peer))
     for j in range(1, m):
         peer = lax.rem(rep + j, m)
-        sent.append(
-            send(mine, grads.at[rep, me], c_send.at[j, 0], c_recv.at[j, 0], "rep", peer)
-        )
-        sent.append(send(total, blocks.at[rep], b_send.at[j], b_recv.at[j], "rep", peer))
+        across[j, 0] = send(mine, grads.at[rep, me], c_send.at[j, 0], c_recv.at[j, 0], "rep", peer)
+        wide.append(send(total, blocks.at[rep], b_send.at[j], b_recv.at[j], "rep", peer))
     for i in range(1, n):
         around[i - 1].wait_recv()
         source = lax.rem(me - i + n, n)
         for j in range(1, m):
             peer = lax.rem(rep + j, m)
-            sent.append(
-                send(grads.at[rep, source], grads.at[rep, source], c_send.at[j, i], c_recv.at[j, i], "rep", peer)
-            )
+            piece = grads.at[rep, source]
+            across[j, i] = send(piece, piece, c_send.at[j, i], c_recv.at[j, i], "rep", peer)
+    for copy in wide:
+        copy.wait()
+    expand(blocks, out)
+
+    def settle(i, carry):
+        source = lax.rem(me - i + n, n)
+        for j in range(1, m):
+            piece = grads.at[rep, source]
+            pltpu.make_async_remote_copy(
+                src_ref=piece, dst_ref=piece, send_sem=c_send.at[j, i], recv_sem=c_recv.at[j, i],
+                device_id={"rep": lax.rem(rep + j, m)}, device_id_type=MESH,
+            ).wait_recv()
+        place_chunk(source, grads, cmap, ready if early else None, spread)
+        return carry
+
+    lax.fori_loop(0, n, settle, 0)
+    lay_out(spread, gradient)
     for copy in around:
         copy.wait_send()
-    for copy in sent:
-        copy.wait()
-
-
-def finish_kernel(blocks, grads, cmap, gradient, out, acc):
-    m, n, _, width = grads.shape
-    span = m * width
-    cams = n * span
-    highs = cams // LOW
-    at = 0
-    for k in range(9):
-        for l in range(k, 9):
-            for r in range(m):
-                row = blocks[r, at : at + 1, :]
-                lanes = slice(r * width, (r + 1) * width)
-                out[k * 9 + l : k * 9 + l + 1, lanes] = row
-                if l != k:
-                    out[l * 9 + k : l * 9 + k + 1, lanes] = row
-            at += 1
-    acc[...] = jnp.zeros_like(acc)
-
-    def body(o, carry):
-        slots = jnp.concatenate([grads[r, o] for r in range(m)], axis=1)
-        ids = cmap[:, pl.ds(pl.multiple_of(o * span, span), span)]
-        up, down = ids // LOW, lax.rem(ids, LOW)
-        one_hot = one_hot_of(down, LOW)
-        high, low = split(slots)
-        top = jnp.concatenate([high[0:8], low[0:8]], axis=0).astype(BF16)
-        up16 = jnp.broadcast_to(up.astype(F32), (16, span)).astype(BF16)
-        none = jnp.zeros_like(top)
-        mask = up == lax.broadcasted_iota(jnp.int32, (highs, span), 0)
-        last = jnp.concatenate([jnp.where(mask, high[8:9], 0.0), jnp.where(mask, low[8:9], 0.0)], axis=0).astype(BF16)
-        dims = (((1,), (1,)), ((), ()))
-        group = min(highs, 32)
-
-        def tiles(start):
-            return [
-                jnp.where(up16 == jnp.asarray(start + h, F32).astype(BF16), top, none) for h in range(group)
-            ]
-
-        if group == highs:
-            lhs = jnp.concatenate(tiles(0) + [last], axis=0)
-            acc[...] += lax.dot_general(lhs, one_hot, dims, preferred_element_type=F32)
-            return carry
-
-        def some(g, carry):
-            lhs = jnp.concatenate(tiles(g * group), axis=0)
-            where = pl.ds(pl.multiple_of(g * group * 16, group * 16), group * 16)
-            acc[where, :] += lax.dot_general(lhs, one_hot, dims, preferred_element_type=F32)
-            return carry
-
-        lax.fori_loop(0, highs // group, some, 0)
-        acc[highs * 16 :, :] += lax.dot_general(last, one_hot, dims, preferred_element_type=F32)
-        return carry
-
-    lax.fori_loop(0, n, body, 0)
-    for h in range(highs):
-        lanes = slice(h * LOW, (h + 1) * LOW)
-        gradient[0:8, lanes] = acc[h * 16 : h * 16 + 8, :] + acc[h * 16 + 8 : h * 16 + 16, :]
-        ninth = highs * 16 + h
-        gradient[8:9, lanes] = acc[ninth : ninth + 1, :] + acc[ninth + highs : ninth + highs + 1, :]
+    for copy in across.values():
+        copy.wait_send()
 
 
 def local(jacobians, residuals, camera_local, bucket_counts, camera_map):
@@ -232,16 +253,20 @@
     width = CAM_DEV // m
     highs = cams // LOW
     limit = 60 * 1024 * 1024
-    params = pltpu.CompilerParams(vmem_limit_bytes=limit)
     dma = pltpu.SemaphoreType.DMA
-    blocks, grads = pl.pallas_call(
+    early = n if n * LOW * CAM_DEV * 2 <= 8 * 1024 * 1024 else 1
+    gradient, out = pl.pallas_call(
         functools.partial(main_kernel, n, m),
-        out_shape=(jax.ShapeDtypeStruct((m, KEPT, width), F32), jax.ShapeDtypeStruct((m, n, 9, width), F32)),
-        in_specs=[pl.BlockSpec(memory_space=pltpu.SMEM)] + [vspec()] * 3,
+        out_shape=(jax.ShapeDtypeStruct((9, cams), F32), jax.ShapeDtypeStruct((81, CAM_DEV), F32)),
+        in_specs=[pl.BlockSpec(memory_space=pltpu.SMEM)] + [vspec()] * 4,
         out_specs=(vspec(), vspec()),
         scratch_shapes=[
-            VMEM((24, slots), F32),
-            VMEM((n, 24, cap), F32),
+            VMEM((m, KEPT, width), F32),
+            VMEM((m, n, 9, width), F32),
+            VMEM((early, LOW, CAM_DEV), BF16),
+            VMEM((highs * 18, LOW), F32),
+            VMEM((21, slots), F32),
+            VMEM((n, 21, cap), F32),
             VMEM((ROWS, cap), F32),
             VMEM((m, ROWS, width), F32),
             VMEM((m, ROWS, width), F32),
@@ -259,15 +284,7 @@
             dma((m, n)),
         ],
         compiler_params=pltpu.CompilerParams(collective_id=0, has_side_effects=True, vmem_limit_bytes=limit),
-    )(bucket_counts, jacobians, residuals, camera_local.reshape(1, slots))
-    gradient, out = pl.pallas_call(
-        finish_kernel,
-        out_shape=(jax.ShapeDtypeStruct((9, cams), F32), jax.ShapeDtypeStruct((81, CAM_DEV), F32)),
-        in_specs=[vspec()] * 3,
-        out_specs=(vspec(), vspec()),
-        scratch_shapes=[VMEM((highs * 18, LOW), F32)],
-        compiler_params=params,
-    )(blocks, grads, camera_map.reshape(1, cams))
+    )(bucket_counts, jacobians, residuals, camera_local.reshape(1, slots), camera_map.reshape(1, cams))
     return (gradient, out)
 
 

time: 41.4 us -> 38.7 us (0.935)
  Pallas kernels: 40.6 us -> 35.2 us
  local copies, waits for them, and re-layouts: 0 us -> 2.66 us
    pallas_call x1 -> x0, Pallas kernels: 6.26 us -> none  [local(): pl.pallas_call(finish_kernel, out_shape=(jax.ShapeDtypeStruct((9, cams),...]
    unnamed x0 -> x4, local copies, waits for them, and re-layouts: none -> 2.66 us
    pallas_call x1, Pallas kernels: 34.4 us -> 35.2 us  [local(): pl.pallas_call(functools.partial(main_kernel, n, m), out_shape=(jax.Shape...]
where the time goes in v4:
time: 38.7 us; the launch traced here: 38.5 us
  Pallas kernels  35.2 us (91%)
  local copies, waits for them, and re-layouts  2.66 us (7%)
  between operations  0.65 us (2%)
    pallas_call x1, Pallas kernels, local(): pl.pallas_call(functools.partial(main_kernel, n, m), out_shape=(jax.Shape...  35.2 us
    unnamed x4, local copies, waits for them, and re-layouts  2.66 us

profile of v4, /device:TPU:0, one launch (start us, length us, event | category | flops | bytes accessed | tf_op | source)
XLA Modules:
  0.0 38.5 jit_solution(11454411540791423503)
XLA Ops:
  0.6 35.2 %shard_map.68 = (f32[9,8192]{1,0:T(8,128)}, f32[81,1024]{1,0:T(8,128)}) custom-call(s32[1,8]{1,0:T(1,128)} %counts.1, f32[18,4096]{1,0:T(8,128)} %jac.1, f32[2,4096]{1,0:T(2,128)} %res.1, s32[1,4096]{1,0:T(1,128)} %bitcast.3, s32[1,8192]{1,0:T(1,128)} %bitcast.2), custom_call_target="tpu_custom_call" | custom-call | tf_op jit(solution)/shard_map/pallas_call | solution.py:258
  35.9 0.0 copy-start
  35.9 1.9 %copy.9 = f32[9,8192]{1,0:T(8,128)} copy(f32[9,8192]{1,0:T(8,128)} %get-tuple-element.4) | data formatting | bytes 589824
  37.8 0.0 copy-done
  37.8 0.7 %copy.10 = f32[81,1024]{1,0:T(8,128)} copy(f32[81,1024]{1,0:T(8,128)S(1)} %copy-done) | data formatting | bytes 663552
Async XLA Ops:
  35.9 1.9 %copy-start = (f32[81,1024]{1,0:T(8,128)S(1)}, f32[81,1024]{1,0:T(8,128)}, u32[]{:S(2)}) copy-start(f32[81,1024]{1,0:T(8,128)} %get-tuple-element.5) | copy-start | bytes 995332

commit v5 on v4

--- a/solution.py
+++ b/solution.py
@@ -245,6 +245,15 @@
         copy.wait_send()
 
 
+def write_kernel(gradient, blocks, gradient_out, blocks_out, gradient_sem, blocks_sem):
+    first = pltpu.make_async_copy(gradient, gradient_out, gradient_sem)
+    second = pltpu.make_async_copy(blocks, blocks_out, blocks_sem)
+    first.start()
+    second.start()
+    first.wait()
+    second.wait()
+
+
 def local(jacobians, residuals, camera_local, bucket_counts, camera_map):
     n, m = lax.axis_size("obs"), lax.axis_size("rep")
     slots = jacobians.shape[1]
@@ -252,9 +261,9 @@
     cams = camera_map.shape[0]
     width = CAM_DEV // m
     highs = cams // LOW
-    limit = 60 * 1024 * 1024
     dma = pltpu.SemaphoreType.DMA
     early = n if n * LOW * CAM_DEV * 2 <= 8 * 1024 * 1024 else 1
+    limit = (24 if early == n else 60) * 1024 * 1024
     gradient, out = pl.pallas_call(
         functools.partial(main_kernel, n, m),
         out_shape=(jax.ShapeDtypeStruct((9, cams), F32), jax.ShapeDtypeStruct((81, CAM_DEV), F32)),
@@ -285,7 +294,16 @@
         ],
         compiler_params=pltpu.CompilerParams(collective_id=0, has_side_effects=True, vmem_limit_bytes=limit),
     )(bucket_counts, jacobians, residuals, camera_local.reshape(1, slots), camera_map.reshape(1, cams))
-    return (gradient, out)
+    anywhere = pl.BlockSpec(memory_space=pl.ANY)
+    shapes = (jax.ShapeDtypeStruct(gradient.shape, F32), jax.ShapeDtypeStruct(out.shape, F32))
+    return pl.pallas_call(
+        write_kernel,
+        out_shape=shapes,
+        in_specs=[anywhere] * 2,
+        out_specs=(anywhere, anywhere),
+        scratch_shapes=[dma, dma],
+        compiler_params=pltpu.CompilerParams(vmem_limit_bytes=limit),
+    )(gradient, out)
 
 
 def solution(mesh):

time: 38.7 us -> 39.6 us (1.023)
  local copies, waits for them, and re-layouts: 2.66 us -> 3.88 us
  Pallas kernels: 35.2 us -> 34.7 us
    pallas_call x1, Pallas kernels: 35.2 us -> 33.8 us  [local(): pl.pallas_call(functools.partial(main_kernel, n, m), out_shape=(jax.Shape...]
    unnamed x4 -> x10, local copies, waits for them, and re-layouts: 2.66 us -> 3.88 us
    pallas_call x0 -> x1, Pallas kernels: none -> 0.93 us  [local(): pl.pallas_call(write_kernel, out_shape=shapes, in_specs=[anywhere] * 2, o...]
where the time goes in v5:
time: 39.6 us; the launch traced here: 39.3 us
  Pallas kernels  34.7 us (88%)
  local copies, waits for them, and re-layouts  3.88 us (10%)
  between operations  0.65 us (2%)
    pallas_call x1, Pallas kernels, local(): pl.pallas_call(functools.partial(main_kernel, n, m), out_shape=(jax.Shape...  33.8 us
    unnamed x10, local copies, waits for them, and re-layouts  3.88 us
    pallas_call x1, Pallas kernels, local(): pl.pallas_call(write_kernel, out_shape=shapes, in_specs=[anywhere] * 2, o...  0.93 us

profile of v5, /device:TPU:0, one launch (start us, length us, event | category | flops | bytes accessed | tf_op | source)
XLA Modules:
  0.0 39.3 jit_solution(347874351969851537)
XLA Ops:
  0.6 0.0 copy-start.4
  0.6 0.6 %copy-done.4 = s32[1,8]{1,0:T(1,128)S(1)} copy-done((s32[1,8]{1,0:T(1,128)S(1)}, s32[1,8]{1,0:T(1,128)}, u32[]{:S(2)}) %copy-start.4) | copy-done | bytes 56
  1.3 0.0 copy-start
  1.3 1.0 %copy-done = f32[18,4096]{1,0:T(8,128)S(1)} copy-done((f32[18,4096]{1,0:T(8,128)S(1)}, f32[18,4096]{1,0:T(8,128)}, u32[]{:S(2)}) %copy-start) | copy-done | bytes 294936
  2.3 0.0 copy-start.1
  2.3 0.8 %copy-done.1 = f32[2,4096]{1,0:T(2,128)S(1)} copy-done((f32[2,4096]{1,0:T(2,128)S(1)}, f32[2,4096]{1,0:T(2,128)}, u32[]{:S(2)}) %copy-start.1) | copy-done | bytes 32792
  3.0 0.0 copy-start.2
  3.0 0.8 %copy-done.2 = s32[8192]{0:T(1024)S(1)} copy-done((s32[8192]{0:T(1024)S(1)}, s32[8192]{0:T(1024)}, u32[]{:S(2)}) %copy-start.2) | copy-done | bytes 32792
  3.8 0.0 copy-start.3
  3.8 0.7 %copy-done.3 = s32[4096]{0:T(1024)S(1)} copy-done((s32[4096]{0:T(1024)S(1)}, s32[4096]{0:T(1024)}, u32[]{:S(2)}) %copy-start.3) | copy-done | bytes 16408
  4.5 33.8 %shard_map.68 = (f32[9,8192]{1,0:T(8,128)S(1)}, f32[81,1024]{1,0:T(8,128)S(1)}) custom-call(s32[1,8]{1,0:T(1,128)S(1)} %copy-done.4, f32[18,4096]{1,0:T(8,128)S(1)} %copy-done, f32[2,4096]{1,0:T(2,128)S(1)} %copy-done.1, s32[1,4096]{1,0:T(1,128)S(1)} %bitcast.3, s32[1,8192]{1,0:T(1,128)S(1)} %bitcast.2), custom_call_target="tpu_custom_call" | custom-call | tf_op jit(solution)/shard_map/pallas_call | solution.py:267
  38.3 0.9 %shard_map.69 = (f32[9,8192]{1,0:T(8,128)}, f32[81,1024]{1,0:T(8,128)}) custom-call(f32[9,8192]{1,0:T(8,128)S(1)} %get-tuple-element.4.gradient, f32[81,1024]{1,0:T(8,128)S(1)} %get-tuple-element.5.blocks), custom_call_target="tpu_custom_call" | custom-call | tf_op jit(solution)/shard_map/pallas_call | solution.py:299
Async XLA Ops:
  0.6 0.7 %copy-start.4 = (s32[1,8]{1,0:T(1,128)S(1)}, s32[1,8]{1,0:T(1,128)}, u32[]{:S(2)}) copy-start(s32[1,8]{1,0:T(1,128)} %counts.1) | copy-start | bytes 100
  1.3 1.0 %copy-start = (f32[18,4096]{1,0:T(8,128)S(1)}, f32[18,4096]{1,0:T(8,128)}, u32[]{:S(2)}) copy-start(f32[18,4096]{1,0:T(8,128)} %jac.1) | copy-start | bytes 884740
  2.3 0.8 %copy-start.1 = (f32[2,4096]{1,0:T(2,128)S(1)}, f32[2,4096]{1,0:T(2,128)}, u32[]{:S(2)}) copy-start(f32[2,4096]{1,0:T(2,128)} %res.1) | copy-start | bytes 98308
  3.0 0.8 %copy-start.2 = (s32[8192]{0:T(1024)S(1)}, s32[8192]{0:T(1024)}, u32[]{:S(2)}) copy-start(s32[8192]{0:T(1024)} %param.9) | copy-start | bytes 98308
  3.8 0.7 %copy-start.3 = (s32[4096]{0:T(1024)S(1)}, s32[4096]{0:T(1024)}, u32[]{:S(2)}) copy-start(s32[4096]{0:T(1024)} %param.7) | copy-start | bytes 49156

commit v6 on v5

--- a/solution.py
+++ b/solution.py
@@ -128,7 +128,7 @@
 
 
 def main_kernel(
-    n, m, counts, jac, res, ids, cmap, gradient, out, blocks, grads, ready, spread, packed, moved, terms, part, landed, total, mine,
+    n, m, counts, jac_in, res_in, ids_in, cmap_in, gradient, out, jac, res, ids, cmap, load_sem, blocks, grads, ready, spread, packed, moved, terms, part, landed, total, mine,
     x_send, x_recv, a_send, a_recv, b_send, b_recv, g_send, g_recv, c_send, c_recv,
 ):
     me, rep = lax.axis_index("obs"), lax.axis_index("rep")
@@ -139,9 +139,16 @@
         pl.semaphore_signal(barrier, inc=1, device_id={"obs": lax.rem(me + i, n)}, device_id_type=MESH)
     for i in range(1, m):
         pl.semaphore_signal(barrier, inc=1, device_id={"rep": lax.rem(rep + i, m)}, device_id_type=MESH)
-    pack(counts, jac, res, ids, packed)
+    pairs = ((jac_in, jac), (res_in, res), (ids_in, ids), (cmap_in, cmap))
+    loads = [pltpu.make_async_copy(src, dst, load_sem.at[k]) for k, (src, dst) in enumerate(pairs)]
+    for load in loads:
+        load.start()
     part[...] = jnp.zeros_like(part)
     terms[...] = jnp.zeros_like(terms)
+    spread[...] = jnp.zeros_like(spread)
+    for load in loads:
+        load.wait()
+    pack(counts, jac, res, ids, packed)
     pl.semaphore_wait(barrier, n + m - 2)
 
     def lanes_of(peer):
@@ -183,7 +190,6 @@
 
     if early:
         lax.fori_loop(0, n, prepare, 0)
-    spread[...] = jnp.zeros_like(spread)
     lax.fori_loop(1, n, take, 0)
 
     def send(src, dst, s, r, axis, peer):
@@ -267,9 +273,14 @@
     gradient, out = pl.pallas_call(
         functools.partial(main_kernel, n, m),
         out_shape=(jax.ShapeDtypeStruct((9, cams), F32), jax.ShapeDtypeStruct((81, CAM_DEV), F32)),
-        in_specs=[pl.BlockSpec(memory_space=pltpu.SMEM)] + [vspec()] * 4,
+        in_specs=[pl.BlockSpec(memory_space=pltpu.SMEM)] + [pl.BlockSpec(memory_space=pltpu.HBM)] * 4,
         out_specs=(vspec(), vspec()),
         scratch_shapes=[
+            VMEM((18, slots), F32),
+            VMEM((2, slots), F32),
+            VMEM((1, slots), jnp.int32),
+            VMEM((1, cams), jnp.int32),
+            dma((4,)),
             VMEM((m, KEPT, width), F32),
             VMEM((m, n, 9, width), F32),
             VMEM((early, LOW, CAM_DEV), BF16),

time: 39.6 us -> 39.6 us (level)
  no operation moved by 1% of the time
where the time goes in v6:
time: 39.6 us; the launch traced here: 39.3 us
  Pallas kernels  34.8 us (88%)
  local copies, waits for them, and re-layouts  3.88 us (10%)
  between operations  0.65 us (2%)
    pallas_call x1, Pallas kernels, local(): pl.pallas_call(functools.partial(main_kernel, n, m), out_shape=(jax.Shape...  33.8 us
    unnamed x10, local copies, waits for them, and re-layouts  3.88 us
    pallas_call x1, Pallas kernels, local(): pl.pallas_call(write_kernel, out_shape=shapes, in_specs=[anywhere] * 2, o...  0.93 us

profile of v6, /device:TPU:0, one launch (start us, length us, event | category | flops | bytes accessed | tf_op | source)
XLA Modules:
  0.0 39.3 jit_solution(10905433129565868520)
XLA Ops:
  0.6 0.0 copy-start.4
  0.6 0.6 %copy-done.4 = s32[1,8]{1,0:T(1,128)S(1)} copy-done((s32[1,8]{1,0:T(1,128)S(1)}, s32[1,8]{1,0:T(1,128)}, u32[]{:S(2)}) %copy-start.4) | copy-done | bytes 56
  1.3 0.0 copy-start
  1.3 1.0 %copy-done = f32[18,4096]{1,0:T(8,128)S(1)} copy-done((f32[18,4096]{1,0:T(8,128)S(1)}, f32[18,4096]{1,0:T(8,128)}, u32[]{:S(2)}) %copy-start) | copy-done | bytes 294936
  2.3 0.0 copy-start.1
  2.3 0.8 %copy-done.1 = f32[2,4096]{1,0:T(2,128)S(1)} copy-done((f32[2,4096]{1,0:T(2,128)S(1)}, f32[2,4096]{1,0:T(2,128)}, u32[]{:S(2)}) %copy-start.1) | copy-done | bytes 32792
  3.0 0.0 copy-start.2
  3.0 0.8 %copy-done.2 = s32[8192]{0:T(1024)S(1)} copy-done((s32[8192]{0:T(1024)S(1)}, s32[8192]{0:T(1024)}, u32[]{:S(2)}) %copy-start.2) | copy-done | bytes 32792
  3.8 0.0 copy-start.3
  3.8 0.7 %copy-done.3 = s32[4096]{0:T(1024)S(1)} copy-done((s32[4096]{0:T(1024)S(1)}, s32[4096]{0:T(1024)}, u32[]{:S(2)}) %copy-start.3) | copy-done | bytes 16408
  4.5 33.8 %shard_map.68 = (f32[9,8192]{1,0:T(8,128)S(1)}, f32[81,1024]{1,0:T(8,128)S(1)}) custom-call(s32[1,8]{1,0:T(1,128)S(1)} %copy-done.4, f32[18,4096]{1,0:T(8,128)S(1)} %copy-done, f32[2,4096]{1,0:T(2,128)S(1)} %copy-done.1, s32[1,4096]{1,0:T(1,128)S(1)} %bitcast.3, s32[1,8192]{1,0:T(1,128)S(1)} %bitcast.2), custom_call_target="tpu_custom_call" | custom-call | tf_op jit(solution)/shard_map/pallas_call | solution.py:273
  38.4 0.9 %shard_map.69 = (f32[9,8192]{1,0:T(8,128)}, f32[81,1024]{1,0:T(8,128)}) custom-call(f32[9,8192]{1,0:T(8,128)S(1)} %get-tuple-element.4.gradient, f32[81,1024]{1,0:T(8,128)S(1)} %get-tuple-element.5.blocks), custom_call_target="tpu_custom_call" | custom-call | tf_op jit(solution)/shard_map/pallas_call | solution.py:310
Async XLA Ops:
  0.6 0.7 %copy-start.4 = (s32[1,8]{1,0:T(1,128)S(1)}, s32[1,8]{1,0:T(1,128)}, u32[]{:S(2)}) copy-start(s32[1,8]{1,0:T(1,128)} %counts.1) | copy-start | bytes 100
  1.3 1.0 %copy-start = (f32[18,4096]{1,0:T(8,128)S(1)}, f32[18,4096]{1,0:T(8,128)}, u32[]{:S(2)}) copy-start(f32[18,4096]{1,0:T(8,128)} %jac_in.1) | copy-start | bytes 884740
  2.3 0.8 %copy-start.1 = (f32[2,4096]{1,0:T(2,128)S(1)}, f32[2,4096]{1,0:T(2,128)}, u32[]{:S(2)}) copy-start(f32[2,4096]{1,0:T(2,128)} %res_in.1) | copy-start | bytes 98308
  3.0 0.8 %copy-start.2 = (s32[8192]{0:T(1024)S(1)}, s32[8192]{0:T(1024)}, u32[]{:S(2)}) copy-start(s32[8192]{0:T(1024)} %param.9) | copy-start | bytes 98308
  3.8 0.7 %copy-start.3 = (s32[4096]{0:T(1024)S(1)}, s32[4096]{0:T(1024)}, u32[]{:S(2)}) copy-start(s32[4096]{0:T(1024)} %param.7) | copy-start | bytes 49156

commit v7 on v6

--- a/solution.py
+++ b/solution.py
@@ -251,13 +251,22 @@
         copy.wait_send()
 
 
-def write_kernel(gradient, blocks, gradient_out, blocks_out, gradient_sem, blocks_sem):
-    first = pltpu.make_async_copy(gradient, gradient_out, gradient_sem)
-    second = pltpu.make_async_copy(blocks, blocks_out, blocks_sem)
-    first.start()
-    second.start()
-    first.wait()
-    second.wait()
+def write_kernel(gradient, blocks, gradient_out, blocks_out, gradient_held, blocks_held, in_sem, out_sem):
+    def cut(ref, count):
+        step = ref.shape[1] // count
+        return [ref.at[:, pl.ds(c * step, step)] for c in range(count)]
+
+    jobs = list(zip(cut(blocks, 2), cut(blocks_held, 2), cut(blocks_out, 2)))
+    jobs += list(zip(cut(gradient, 4), cut(gradient_held, 4), cut(gradient_out, 4)))
+    reads = [pltpu.make_async_copy(job[0], job[1], in_sem.at[j]) for j, job in enumerate(jobs)]
+    writes = [pltpu.make_async_copy(job[1], job[2], out_sem.at[j]) for j, job in enumerate(jobs)]
+    for read in reads:
+        read.start()
+    for read, write in zip(reads, writes):
+        read.wait()
+        write.start()
+    for write in writes:
+        write.wait()
 
 
 def local(jacobians, residuals, camera_local, bucket_counts, camera_map):
@@ -269,7 +278,7 @@
     highs = cams // LOW
     dma = pltpu.SemaphoreType.DMA
     early = n if n * LOW * CAM_DEV * 2 <= 8 * 1024 * 1024 else 1
-    limit = (24 if early == n else 60) * 1024 * 1024
+    limit = 60 * 1024 * 1024
     gradient, out = pl.pallas_call(
         functools.partial(main_kernel, n, m),
         out_shape=(jax.ShapeDtypeStruct((9, cams), F32), jax.ShapeDtypeStruct((81, CAM_DEV), F32)),
@@ -312,7 +321,7 @@
         out_shape=shapes,
         in_specs=[anywhere] * 2,
         out_specs=(anywhere, anywhere),
-        scratch_shapes=[dma, dma],
+        scratch_shapes=[VMEM(gradient.shape, F32), VMEM(out.shape, F32), dma((6,)), dma((6,))],
         compiler_params=pltpu.CompilerParams(vmem_limit_bytes=limit),
     )(gradient, out)
 

time: 39.6 us -> 37.7 us (0.952)
  local copies, waits for them, and re-layouts: 3.88 us -> 0 us
  Pallas kernels: 34.8 us -> 36.9 us
    unnamed x10 -> x0, local copies, waits for them, and re-layouts: 3.88 us -> none
    pallas_call x1, Pallas kernels: 0.93 us -> 2.01 us  [local(): pl.pallas_call(write_kernel, out_shape=shapes, in_specs=[anywhere] * 2, o...]
    pallas_call x1, Pallas kernels: 33.8 us -> 34.9 us  [local(): pl.pallas_call(functools.partial(main_kernel, n, m), out_shape=(jax.Shape...]
where the time goes in v7:
time: 37.7 us; the launch traced here: 37.5 us
  Pallas kernels  36.9 us (98%)
  between operations  0.64 us (2%)
    pallas_call x1, Pallas kernels, local(): pl.pallas_call(functools.partial(main_kernel, n, m), out_shape=(jax.Shape...  34.9 us
    pallas_call x1, Pallas kernels, local(): pl.pallas_call(write_kernel, out_shape=shapes, in_specs=[anywhere] * 2, o...  2.01 us

profile of v7, /device:TPU:0, one launch (start us, length us, event | category | flops | bytes accessed | tf_op | source)
XLA Modules:
  0.0 37.5 jit_solution(3687551786058145009)
XLA Ops:
  0.6 34.9 %shard_map.68 = (f32[9,8192]{1,0:T(8,128)}, f32[81,1024]{1,0:T(8,128)}) custom-call(s32[1,8]{1,0:T(1,128)} %counts.1, f32[18,4096]{1,0:T(8,128)} %jac_in.1, f32[2,4096]{1,0:T(2,128)} %res_in.1, s32[1,4096]{1,0:T(1,128)} %bitcast.3, s32[1,8192]{1,0:T(1,128)} %bitcast.2), custom_call_target="tpu_custom_call" | custom-call | tf_op jit(solution)/shard_map/pallas_call | solution.py:282
  35.5 2.0 %shard_map.69 = (f32[9,8192]{1,0:T(8,128)}, f32[81,1024]{1,0:T(8,128)}) custom-call(f32[9,8192]{1,0:T(8,128)} %get-tuple-element.4.gradient, f32[81,1024]{1,0:T(8,128)} %get-tuple-element.5.blocks), custom_call_target="tpu_custom_call" | custom-call | tf_op jit(solution)/shard_map/pallas_call | solution.py:319

commit v8 on v7

--- a/solution.py
+++ b/solution.py
@@ -13,7 +13,7 @@
 BF16 = jnp.bfloat16
 VMEM = pltpu.VMEM
 ROWS = 56
-GRAD = 45
+HEAD = 16
 KEPT = 48
 LOW = 256
 
@@ -49,11 +49,11 @@
     cap = block.shape[1]
     lead, trail, res = block[0:9], block[9:18], block[18:20]
     ids = block[20:21].astype(jnp.int32)
-    at = 0
+    at = 9
     for k in range(9):
         terms[at : at + 9 - k, :] = lead[k : k + 1] * lead[k:9] + trail[k : k + 1] * trail[k:9]
         at += 9 - k
-    terms[GRAD : GRAD + 9, :] = lead * res[0:1] + trail * res[1:2]
+    terms[0:9, :] = lead * res[0:1] + trail * res[1:2]
     high, low = split(terms[...])
     both = jnp.concatenate([high, low], axis=0).astype(BF16)
     pieces, _, width = acc.shape
@@ -71,7 +71,7 @@
 
 def expand(blocks, out):
     m, _, width = blocks.shape
-    at = 0
+    at = 1
     for k in range(9):
         for l in range(k, 9):
             for r in range(m):
@@ -199,20 +199,20 @@
         copy.start()
         return copy
 
-    first = []
+    first, second = [], []
+    for half, rows, copies in ((0, pl.ds(0, HEAD), first), (1, pl.ds(HEAD, ROWS - HEAD), second)):
+        for i in range(1, m):
+            peer = lax.rem(rep + i, m)
+            copies.append(
+                send(part.at[peer, rows], landed.at[i, rows], a_send.at[half, i], a_recv.at[half, i], "rep", peer)
+            )
+    for copy in first:
+        copy.wait_recv()
+    head = part[rep, 0:HEAD]
     for i in range(1, m):
-        peer = lax.rem(rep + i, m)
-        first.append(send(part.at[peer], landed.at[i], a_send.at[i], a_recv.at[i], "rep", peer))
-    lax.fori_loop(1, n, drain, 0)
-    own = part[rep]
-    for copy in first:
-        copy.wait()
-    for i in range(1, m):
-        own = own + landed[i]
-    total[...] = own[:KEPT]
-    mine[...] = own[GRAD : GRAD + 9]
-    grads[rep, me] = own[GRAD : GRAD + 9]
-    blocks[rep] = own[:KEPT]
+        head = head + landed[i, 0:HEAD]
+    mine[...] = head[0:9]
+    grads[rep, me] = head[0:9]
     around, wide, across = [], [], {}
     for i in range(1, n):
         peer = lax.rem(me + i, n)
@@ -220,7 +220,19 @@
     for j in range(1, m):
         peer = lax.rem(rep + j, m)
         across[j, 0] = send(mine, grads.at[rep, me], c_send.at[j, 0], c_recv.at[j, 0], "rep", peer)
+    for copy in second:
+        copy.wait_recv()
+    rest = part[rep, ROWS - KEPT : ROWS]
+    for i in range(1, m):
+        rest = rest + landed[i, ROWS - KEPT : ROWS]
+    total[...] = rest
+    blocks[rep] = rest
+    for j in range(1, m):
+        peer = lax.rem(rep + j, m)
         wide.append(send(total, blocks.at[rep], b_send.at[j], b_recv.at[j], "rep", peer))
+    for copy in first + second:
+        copy.wait_send()
+    lax.fori_loop(1, n, drain, 0)
     for i in range(1, n):
         around[i - 1].wait_recv()
         source = lax.rem(me - i + n, n)
@@ -303,8 +315,8 @@
             VMEM((9, width), F32),
             dma((n,)),
             dma((n,)),
-            dma((m,)),
-            dma((m,)),
+            dma((2, m)),
+            dma((2, m)),
             dma((m,)),
             dma((m,)),
             dma((n,)),

time: 37.7 us -> 36.9 us (0.979)
  Pallas kernels: 36.9 us -> 36.1 us
    pallas_call x1, Pallas kernels: 34.9 us -> 34 us  [local(): pl.pallas_call(functools.partial(main_kernel, n, m), out_shape=(jax.Shape...]
where the time goes in v8:
time: 36.9 us; the launch traced here: 36.7 us
  Pallas kernels  36.1 us (98%)
  between operations  0.64 us (2%)
    pallas_call x1, Pallas kernels, local(): pl.pallas_call(functools.partial(main_kernel, n, m), out_shape=(jax.Shape...  34 us
    pallas_call x1, Pallas kernels, local(): pl.pallas_call(write_kernel, out_shape=shapes, in_specs=[anywhere] * 2, o...  2.01 us

profile of v8, /device:TPU:0, one launch (start us, length us, event | category | flops | bytes accessed | tf_op | source)
XLA Modules:
  0.0 36.7 jit_solution(12532392111751617750)
XLA Ops:
  0.6 34.0 %shard_map.68 = (f32[9,8192]{1,0:T(8,128)}, f32[81,1024]{1,0:T(8,128)}) custom-call(s32[1,8]{1,0:T(1,128)} %counts.1, f32[18,4096]{1,0:T(8,128)} %jac_in.1, f32[2,4096]{1,0:T(2,128)} %res_in.1, s32[1,4096]{1,0:T(1,128)} %bitcast.3, s32[1,8192]{1,0:T(1,128)} %bitcast.2), custom_call_target="tpu_custom_call" | custom-call | tf_op jit(solution)/shard_map/pallas_call | solution.py:294
  34.7 2.0 %shard_map.69 = (f32[9,8192]{1,0:T(8,128)}, f32[81,1024]{1,0:T(8,128)}) custom-call(f32[9,8192]{1,0:T(8,128)} %get-tuple-element.4.gradient, f32[81,1024]{1,0:T(8,128)} %get-tuple-element.5.blocks), custom_call_target="tpu_custom_call" | custom-call | tf_op jit(solution)/shard_map/pallas_call | solution.py:331

commit v9 on v8

--- a/solution.py
+++ b/solution.py
@@ -255,7 +255,7 @@
         place_chunk(source, grads, cmap, ready if early else None, spread)
         return carry
 
-    lax.fori_loop(0, n, settle, 0)
+    lax.fori_loop(0, n, settle, 0, unroll=2)
     lay_out(spread, gradient)
     for copy in around:
         copy.wait_send()

time: 36.9 us -> 38.5 us (1.043)
  Pallas kernels: 36.1 us -> 37.7 us
    pallas_call x1, Pallas kernels: 34 us -> 35.6 us  [local(): pl.pallas_call(functools.partial(main_kernel, n, m), out_shape=(jax.Shape...]
where the time goes in v9:
time: 38.5 us; the launch traced here: 38.3 us
  Pallas kernels  37.7 us (98%)
  between operations  0.64 us (2%)
    pallas_call x1, Pallas kernels, local(): pl.pallas_call(functools.partial(main_kernel, n, m), out_shape=(jax.Shape...  35.6 us
    pallas_call x1, Pallas kernels, local(): pl.pallas_call(write_kernel, out_shape=shapes, in_specs=[anywhere] * 2, o...  2.01 us

profile of v9, /device:TPU:0, one launch (start us, length us, event | category | flops | bytes accessed | tf_op | source)
XLA Modules:
  0.0 38.3 jit_solution(807317499414011689)
XLA Ops:
  0.6 35.6 %shard_map.68 = (f32[9,8192]{1,0:T(8,128)}, f32[81,1024]{1,0:T(8,128)}) custom-call(s32[1,8]{1,0:T(1,128)} %counts.1, f32[18,4096]{1,0:T(8,128)} %jac_in.1, f32[2,4096]{1,0:T(2,128)} %res_in.1, s32[1,4096]{1,0:T(1,128)} %bitcast.3, s32[1,8192]{1,0:T(1,128)} %bitcast.2), custom_call_target="tpu_custom_call" | custom-call | tf_op jit(solution)/shard_map/pallas_call | solution.py:294
  36.3 2.0 %shard_map.69 = (f32[9,8192]{1,0:T(8,128)}, f32[81,1024]{1,0:T(8,128)}) custom-call(f32[9,8192]{1,0:T(8,128)} %get-tuple-element.4.gradient, f32[81,1024]{1,0:T(8,128)} %get-tuple-element.5.blocks), custom_call_target="tpu_custom_call" | custom-call | tf_op jit(solution)/shard_map/pallas_call | solution.py:331
